TPU v7x, 32 devices: a whole 2x2x4 slice. The times are simulated.
32 devices in a mesh: tm: 8 (over z, x), clip: 4 (over y, core).
Axes of the slice: x: 2, y: 2, z: 4, core: 2. Of those that a mesh axis runs over, the one named last changes fastest.
Arguments:
- video: float32 [4, 8, 16, 32, 320], P('clip', 'tm'), may hold values from -6 to 6
- spatial_w: bfloat16 [9, 320, 320], P(None, 'clip'), may hold values from -0.109375 to 0.109375
- spatial_b: float32 [320], replicated, may hold values from -3 to 3
- temporal_w: float32 [3, 320, 320], P(None, 'clip'), may hold values from -0.1875 to 0.1875
- cotangent: float32 [4, 8, 16, 32, 320], P('clip', 'tm'), may hold values from -6 to 6
Outputs:
- output: float32 [4, 8, 16, 32, 320], P('clip', 'tm')
- grad_video: float32 [4, 8, 16, 32, 320], P('clip', 'tm')
- grad_temporal: float32 [3, 320, 320], P(None, 'clip')
All inputs are finite; a program needn't handle non-finite values.
Results may differ from a plain program's by a relative error of at most 0.0049.
Values may be sent and summed in bfloat16 or wider, within the bound.
A program may use at most 64 MiB of HBM per device.

v0:
```python
import math
import jax
import jax.numpy as jnp
from jax import lax
from jax.sharding import PartitionSpec as P


def padded_2(cells, sides, width):
    for axis, dim in sides:
        count = lax.axis_size(axis)
        ends = count - 1
        head = lax.slice_in_dim(cells, 0, width, axis=dim)
        tail = lax.slice_in_dim(cells, cells.shape[dim] - width, cells.shape[dim], axis=dim)
        cells = jnp.concatenate(
            [
                lax.ppermute(tail, axis, [(i, (i + 1) % count) for i in range(ends)]),
                cells,
                lax.ppermute(head, axis, [((i + 1) % count, i) for i in range(ends)]),
            ],
            axis=dim,
        )
    return cells


def outer_dot(left, right):
    return lax.dot_general(
        left, right, (((0,), (0,)), ((), ())), preferred_element_type=jnp.float32
    )


def transpose_dot(left, right):
    return lax.dot_general(
        left, right, (((1,), (1,)), ((), ())), preferred_element_type=jnp.float32
    )


def on_device(video, spatial_w, spatial_b, temporal_w, cotangent):
    clips, frames, height, width, chans = video.shape
    row_count = clips * frames * height * width
    video_b = video.astype(jnp.bfloat16)
    padded = jnp.pad(video_b, ((0, 0), (0, 0), (1, 1), (1, 1), (0, 0)))
    temporal_b = temporal_w.astype(jnp.bfloat16)
    spatial_all, temporal_all = (
        lax.all_gather(spatial_w, "clip", axis=1, tiled=True),
        lax.all_gather(temporal_b, "clip", axis=1, tiled=True),
    )
    spatial = jnp.zeros((row_count, chans), jnp.float32)
    for shift_y in range(3):
        for shift_x in range(3):
            window = padded[:, :, shift_y : shift_y + height, shift_x : shift_x + width, :].reshape(
                row_count, chans
            )
            spatial = spatial + jnp.dot(
                window, spatial_all[3 * shift_y + shift_x], preferred_element_type=jnp.float32
            )
    spatial = spatial + spatial_b
    sigmoid_s = jax.nn.sigmoid(spatial)
    hidden = (spatial * sigmoid_s).astype(jnp.bfloat16).reshape(clips, frames, height, width, chans)
    hidden_pad = padded_2(hidden, (("tm", 1),), 1)
    temporal = jnp.zeros((row_count, chans), jnp.float32)
    for kernel_tap in range(3):
        shifted = hidden_pad[:, kernel_tap : kernel_tap + frames].reshape(row_count, chans)
        temporal = temporal + jnp.dot(
            shifted, temporal_all[kernel_tap], preferred_element_type=jnp.float32
        )
    output = video + temporal.reshape(video.shape)
    cot_b = cotangent.astype(jnp.bfloat16)
    cot_flat = cot_b.reshape(row_count, chans)
    cot_pad = padded_2(cot_b, (("tm", 1),), 1)
    grad_hidden = jnp.zeros((row_count, chans), jnp.float32)
    grads = []
    for kernel_tap in range(3):
        shifted_cot = cot_pad[:, 2 - kernel_tap : 2 - kernel_tap + frames].reshape(row_count, chans)
        grad_hidden = grad_hidden + transpose_dot(shifted_cot, temporal_all[kernel_tap])
        shifted_hid = hidden_pad[:, kernel_tap : kernel_tap + frames].reshape(row_count, chans)
        grads.append(outer_dot(shifted_hid, cot_flat))
    local_grad = jnp.stack(grads)
    total_rows = row_count * lax.axis_size("tm") * lax.axis_size("clip")
    summed = lax.psum(local_grad, "tm")
    owned = lax.psum_scatter(summed, "clip", scatter_dimension=1, tiled=True)
    grad_temporal = owned * (1.0 / math.sqrt(total_rows))
    grad_spatial = (grad_hidden * sigmoid_s * (1.0 + spatial * (1.0 - sigmoid_s))).astype(
        jnp.bfloat16
    )
    grad_frames = jnp.pad(
        grad_spatial.reshape(clips, frames, height, width, chans),
        ((0, 0), (0, 0), (1, 1), (1, 1), (0, 0)),
    )
    grad_acc = cotangent.reshape(row_count, chans)
    for shift_y in range(3):
        for shift_x in range(3):
            window = grad_frames[
                :, :, 2 - shift_y : 2 - shift_y + height, 2 - shift_x : 2 - shift_x + width, :
            ].reshape(row_count, chans)
            grad_acc = grad_acc + transpose_dot(window, spatial_all[3 * shift_y + shift_x])
    grad_video = grad_acc.reshape(video.shape)
    return (output, grad_video, grad_temporal)


def solution(mesh):
    return jax.shard_map(
        on_device,
        mesh=mesh,
        in_specs=(
            P("clip", "tm", None, None, None),
            P(None, "clip", None),
            P(),
            P(None, "clip", None),
            P("clip", "tm", None, None, None),
        ),
        out_specs=(
            P("clip", "tm", None, None, None),
            P("clip", "tm", None, None, None),
            P(None, "clip", None),
        ),
        check_vma=False,
    )
```

profile of v0, /device:TPU:0, one launch (start us, length us, event | category | flops | bytes accessed | tf_op | source)
XLA Modules:
  0.0 184.8 jit_solution(11059689400053077663)
XLA Ops:
  9.2 4.9 %collective-permute-start.3 = (bf16[1,1,16,32,320]{4,3,2,1,0:T(8,128)(2,1)S(1)}, bf16[1,1,16,32,320]{4,3,2,1,0:T(8,128)(2,1)S(1)}, u32[]{:S(2)}, u32[]{:S(2)}) collective-permute-start(bf16[1,1,16,32,320]{4,3,2,1,0:T(8,128)(2,1)S(1)} %convert_element_type.21), channel_id=1, source_target_pairs={{0,4},{4,8},{8,12},{12,16},{16,20},{20,24},{24,28},{1,5},{5,9},{9,... | collective-permute-start | bytes 983048 | tf_op jit(solution)/shard_map/ppermute | solution.py:16
  15.5 10.1 %all_gather.7 = bf16[3,320,320]{2,1,0:T(8,128)(2,1)S(1)} all-gather(bf16[3,80,320]{2,1,0:T(8,128)(2,1)S(1)} %convert_element_type.20), channel_id=1, replica_groups=mesh['tm'=8,'clip'=4] {'clip'}, dimensions={1}, use_global_device_ids=true | all-gather | bytes 768000 | tf_op jit(solution)/shard_map/all_gather | solution.py:45
  25.6 1.8 pad_slice_fusion.8
  32.0 4.5 %all-gather.2.cloned.1.call-done = bf16[9,320,320]{2,1,0:T(8,128)(2,1)} async-done(((bf16[9,80,320]{2,1,0:T(8,128)(2,1)}), bf16[9,320,320]{2,1,0:T(8,128)(2,1)}) %all-gather.2.cloned.1.call-update) | async-done | bytes 1843216 | tf_op jit(solution)/shard_map/all_gather | solution.py:44
  36.5 1.6 fusion.14
  38.1 1.5 convolution_add_fusion.14
  39.6 1.4 convolution_add_fusion.13
  43.4 1.4 multiply_convert_fusion
  44.8 1.9 %copy.13 = bf16[512,320]{1,0:T(8,128)(2,1)} copy(bf16[512,320]{0,1:T(8,128)(2,1)} %get-tuple-element.22) | data formatting | bytes 655360 | tf_op jit(solution)/shard_map/convert_element_type | solution.py:58
  48.0 5.9 %collective-permute-start = (bf16[1,1,16,32,320]{4,3,2,1,0:T(8,128)(2,1)}, bf16[1,1,16,32,320]{4,3,2,1,0:T(8,128)(2,1)}, u32[]{:S(2)}, u32[]{:S(2)}) collective-permute-start(bf16[1,1,16,32,320]{4,3,2,1,0:T(8,128)(2,1)} %bitcast.146), channel_id=1, source_target_pairs={{0,4},{4,8},{8,12},{12,16},{16,20},{20,24},{24,28},{1,5},{5,9},{9,... | collective-permute-start | bytes 983048 | tf_op jit(solution)/shard_map/ppermute | solution.py:16
  53.9 2.8 %fusion.9 = bf16[512,320]{0,1:T(8,128)(2,1)} fusion(f32[512,320]{0,1:T(8,128)} %fusion.21, f32[512,320]{0,1:T(8,128)} %fusion.19, bf16[512,320]{1,0:T(8,128)(2,1)} %bitcast.26, f32[512,320]{0,1:T(8,128)} %get-tuple-element.23, bf16[3,320,320]{2,1,0:T(8,128)(2,1)S(1)} %all_gather.7), kind=kOutput, calls=%fused_computation.25 | convolution fusion | flops 106659840 | bytes 2867200 | tf_op jit(solution)/shard_map/dot_general | solution.py:32
  56.7 1.9 %copy.15 = bf16[512,320]{1,0:T(8,128)(2,1)} copy(bf16[512,320]{0,1:T(8,128)(2,1)} %fusion.9) | data formatting | bytes 655360 | tf_op jit(solution)/shard_map/convert_element_type | solution.py:82
  58.6 4.4 %pad_slice_fusion.4 = (bf16[1,1,16,32,320]{4,3,2,1,0:T(8,128)(2,1)}, bf16[1,1,16,32,320]{4,3,2,1,0:T(8,128)(2,1)}, bf16[1,1,16,32,320]{4,3,2,1,0:T(8,128)(2,1)},...) fusion(bf16[1,1,16,32,320]{4,3,2,1,0:T(8,128)(2,1)} %bitcast.132), kind=kLoop, calls=%fused_computation.35 | loop fusion | bytes 2949120 | tf_op jit(solution)/shard_map/slice | solution.py:92
  64.6 1.4 convolution_bitcast_fusion
  66.0 3.7 %collective-permute-done = bf16[1,1,16,32,320]{4,3,2,1,0:T(8,128)(2,1)} collective-permute-done((bf16[1,1,16,32,320]{4,3,2,1,0:T(8,128)(2,1)}, bf16[1,1,16,32,320]{4,3,2,1,0:T(8,128)(2,1)}, u32[]{:S(2)}, u32[]{:S(2)}) %collective-permute-start) | collective-permute-done | bytes 327712 | tf_op jit(solution)/shard_map/ppermute | solution.py:16
  69.6 1.3 convolution_bitcast_fusion.2
  72.3 1.4 fusion.16
  73.8 1.4 fusion.17
  78.9 2.3 %copy.17 = f32[512,320]{1,0:T(8,128)} copy(f32[512,320]{0,1:T(8,128)} %fusion.3) | data formatting | bytes 1310720 | tf_op jit(solution)/shard_map/add | solution.py:95
  81.5 20.0 %reduce-scatter.2.cloned.1.call-done = f32[3,80,320]{2,1,0:T(8,128)} async-done(((f32[3,320,320]{2,1,0:T(8,128)}), f32[3,80,320]{2,1,0:T(8,128)}) %reduce-scatter.2.cloned.1.call-update) | async-done | bytes 307216 | tf_op jit(solution)/shard_map/reduce_scatter | solution.py:80
  101.6 1.4 fusion.22
  103.0 2.3 %fusion.7 = f32[512,320]{0,1:T(8,128)} fusion(f32[512,320]{0,1:T(8,128)S(1)} %fusion.22, f32[512,320]{0,1:T(8,128)S(1)} %fusion.20, bf16[512,320]{1,0:T(8,128)(2,1)} %bitcast.19, bf16[3,320,320]{2,1,0:T(8,128)(2,1)S(1)} %all_gather.7), kind=kOutput, calls=%fused_computation.15 | convolution fusion | flops 105185280 | bytes 2539520 | tf_op jit(solution)/shard_map/dot_general | solution.py:63
  107.6 69.0 %all-reduce.4.cloned.1.call-done = f32[3,80,320]{2,1,0:T(8,128)} async-done(((f32[3,80,320]{2,1,0:T(8,128)}), f32[3,80,320]{2,1,0:T(8,128)}) %all-reduce.4.cloned.1.call-update) | async-done | bytes 307216 | tf_op jit(solution)/shard_map/psum | solution.py:79
  176.5 1.7 broadcast_multiply_fusion
  (80 shorter events, 20.7 us)
Async XLA Ops:
  7.2 8.2 %copy-start.4 = (f32[1,1,16,32,320]{4,3,2,1,0:T(8,128)S(1)}, f32[1,1,16,32,320]{4,3,2,1,0:T(8,128)}, u32[]{:S(2)}) copy-start(f32[1,1,16,32,320]{4,3,2,1,0:T(8,128)} %param.5) | copy-start | bytes 1966084
  7.2 8.2 %copy-start.21 = (f32[3,80,320]{2,1,0:T(8,128)S(1)}, f32[3,80,320]{2,1,0:T(8,128)}, u32[]{:S(2)}) copy-start(f32[3,80,320]{2,1,0:T(8,128)} %param.8) | copy-start | bytes 921604
  7.2 29.3 %all-gather.2.cloned.1.call-start = ((), (), s32[]{:S(2)}) async-start(), calls=%async_computation.1 | async-start | bytes 2764800 | tf_op jit(solution)/shard_map/all_gather | solution.py:44
  7.9 93.6 %reduce-scatter.2.cloned.1.call-start = ((), (), s32[]{:S(2)}) async-start(), calls=%async_computation.2 | async-start | bytes 1843200 | tf_op jit(solution)/shard_map/reduce_scatter | solution.py:80
  9.2 21.7 %collective-permute-start.3 = (bf16[1,1,16,32,320]{4,3,2,1,0:T(8,128)(2,1)S(1)}, bf16[1,1,16,32,320]{4,3,2,1,0:T(8,128)(2,1)S(1)}, u32[]{:S(2)}, u32[]{:S(2)}) collective-permute-start(bf16[1,1,16,32,320]{4,3,2,1,0:T(8,128)(2,1)S(1)} %convert_element_type.21), channel_id=1, source_target_pairs={{0,4},{4,8},{8,12},{12,16},{16,20},{20,24},{24,28},{1,5},{5,9},{9,... | collective-permute-start | bytes 983048 | tf_op jit(solution)/shard_map/ppermute | solution.py:16
  14.1 39.9 %collective-permute-start.2 = (bf16[1,1,16,32,320]{4,3,2,1,0:T(8,128)(2,1)S(1)}, bf16[1,1,16,32,320]{4,3,2,1,0:T(8,128)(2,1)}, u32[]{:S(2)}, u32[]{:S(2)}) collective-permute-start(bf16[1,1,16,32,320]{4,3,2,1,0:T(8,128)(2,1)S(1)} %convert_element_type.21), channel_id=1, source_target_pairs={{4,0},{8,4},{12,8},{16,12},{20,16},{24,20},{28,24},{5,1},{9,5},{13... | collective-permute-start | bytes 983048 | tf_op jit(solution)/shard_map/ppermute | solution.py:18
  15.4 11.9 %copy-start.1 = (bf16[1,1,16,32,320]{4,3,2,1,0:T(8,128)(2,1)}, bf16[1,1,16,32,320]{4,3,2,1,0:T(8,128)(2,1)S(1)}, u32[]{:S(2)}) copy-start(bf16[1,1,16,32,320]{4,3,2,1,0:T(8,128)(2,1)S(1)} %convert_element_type.18) | copy-start | bytes 983044
  15.5 11.9 %copy-start.3 = (f32[1,1,16,32,320]{4,3,2,1,0:T(8,128)S(1)}, f32[1,1,16,32,320]{4,3,2,1,0:T(8,128)}, u32[]{:S(2)}) copy-start(f32[1,1,16,32,320]{4,3,2,1,0:T(8,128)} %param.9) | copy-start | bytes 1966084
  36.5 3.1 %copy-start = (bf16[9,320,320]{2,1,0:T(8,128)(2,1)S(1)}, bf16[9,320,320]{2,1,0:T(8,128)(2,1)}, u32[]{:S(2)}) copy-start(bf16[9,320,320]{2,1,0:T(8,128)(2,1)} %all-gather.2.cloned.1.call-done) | copy-start | bytes 5529604
  38.1 3.0 %copy-start.18 = (bf16[1,1,16,32,320]{4,3,2,1,0:T(8,128)(2,1)S(1)}, bf16[1,1,16,32,320]{4,3,2,1,0:T(8,128)(2,1)}, u32[]{:S(2)}) copy-start(bf16[1,1,16,32,320]{4,3,2,1,0:T(8,128)(2,1)} %get-tuple-element.17) | copy-start | bytes 983044
  39.6 1.9 %copy-start.2 = (bf16[1,1,16,32,320]{4,3,2,1,0:T(8,128)(2,1)S(1)}, bf16[1,1,16,32,320]{4,3,2,1,0:T(8,128)(2,1)}, u32[]{:S(2)}) copy-start(bf16[1,1,16,32,320]{4,3,2,1,0:T(8,128)(2,1)} %copy-done.1) | copy-start | bytes 983044
  41.8 1.1 copy-start.15
  46.7 17.9 %collective-permute-start.1 = (bf16[1,1,16,32,320]{4,3,2,1,0:T(8,128)(2,1)}, bf16[1,1,16,32,320]{4,3,2,1,0:T(8,128)(2,1)}, u32[]{:S(2)}, u32[]{:S(2)}) collective-permute-start(bf16[1,1,16,32,320]{4,3,2,1,0:T(8,128)(2,1)} %bitcast.145), channel_id=1, source_target_pairs={{4,0},{8,4},{12,8},{16,12},{20,16},{24,20},{28,24},{5,1},{9,5},{13... | collective-permute-start | bytes 983048 | tf_op jit(solution)/shard_map/ppermute | solution.py:18
  48.0 21.6 %collective-permute-start = (bf16[1,1,16,32,320]{4,3,2,1,0:T(8,128)(2,1)}, bf16[1,1,16,32,320]{4,3,2,1,0:T(8,128)(2,1)}, u32[]{:S(2)}, u32[]{:S(2)}) collective-permute-start(bf16[1,1,16,32,320]{4,3,2,1,0:T(8,128)(2,1)} %bitcast.146), channel_id=1, source_target_pairs={{0,4},{4,8},{8,12},{12,16},{16,20},{20,24},{24,28},{1,5},{5,9},{9,... | collective-permute-start | bytes 983048 | tf_op jit(solution)/shard_map/ppermute | solution.py:16
  58.6 5.6 %copy-start.6 = (bf16[512,320]{0,1:T(8,128)(2,1)S(1)}, bf16[512,320]{0,1:T(8,128)(2,1)}, u32[]{:S(2)}) copy-start(bf16[512,320]{0,1:T(8,128)(2,1)} %get-tuple-element.22) | copy-start | bytes 983044
  72.2 3.0 %copy-start.10 = (bf16[1,1,16,32,320]{4,3,2,1,0:T(8,128)(2,1)S(1)}, bf16[1,1,16,32,320]{4,3,2,1,0:T(8,128)(2,1)}, u32[]{:S(2)}) copy-start(bf16[1,1,16,32,320]{4,3,2,1,0:T(8,128)(2,1)} %get-tuple-element.12) | copy-start | bytes 983044
  72.3 104.3 %all-reduce.4.cloned.1.call-start = ((), (), s32[]{:S(2)}) async-start(), calls=%async_computation.3 | async-start | bytes 737280 | tf_op jit(solution)/shard_map/psum | solution.py:79
  72.3 3.3 %copy-start.9 = (f32[512,320]{0,1:T(8,128)S(1)}, f32[512,320]{0,1:T(8,128)}, u32[]{:S(2)}) copy-start(f32[512,320]{0,1:T(8,128)} %copy.16) | copy-start | bytes 1966084
  72.3 3.3 %copy-start.14 = (bf16[1,1,16,32,320]{4,3,2,1,0:T(8,128)(2,1)S(1)}, bf16[1,1,16,32,320]{4,3,2,1,0:T(8,128)(2,1)}, u32[]{:S(2)}) copy-start(bf16[1,1,16,32,320]{4,3,2,1,0:T(8,128)(2,1)} %get-tuple-element.13) | copy-start | bytes 983044
  73.8 2.2 %copy-start.13 = (bf16[1,1,16,32,320]{4,3,2,1,0:T(8,128)(2,1)S(1)}, bf16[1,1,16,32,320]{4,3,2,1,0:T(8,128)(2,1)}, u32[]{:S(2)}) copy-start(bf16[1,1,16,32,320]{4,3,2,1,0:T(8,128)(2,1)} %get-tuple-element.7) | copy-start | bytes 983044
  76.4 1.1 copy-start.8
  76.4 1.2 copy-start.19
  77.6 3.5 %copy-start.7 = (bf16[512,320]{0,1:T(8,128)(2,1)S(1)}, bf16[512,320]{0,1:T(8,128)(2,1)}, u32[]{:S(2)}) copy-start(bf16[512,320]{0,1:T(8,128)(2,1)} %get-tuple-element.22) | copy-start | bytes 983044
  102.9 3.7 %copy-start.5 = (f32[1,1,16,32,320]{4,3,2,1,0:T(8,128)S(1)}, f32[1,1,16,32,320]{4,3,2,1,0:T(8,128)}, u32[]{:S(2)}) copy-start(f32[1,1,16,32,320]{4,3,2,1,0:T(8,128)} %param.5) | copy-start | bytes 1966084
  (6 other events, 6.1 us)
Sparse Core Ops, SparseCore 0:
  9.6 26.8 all-gather.1
  72.4 29.1 reduce-scatter.1
  104.9 71.5 all-reduce.3
where the time goes:
time: 186 us; the launch traced here: 185 us
  waiting for transfers between devices  99 us (53%)
  matrix products  27.1 us (15%)
  local copies, waits for them, and re-layouts  15.7 us (8%)
  between operations  14.2 us (8%)
  starting transfers between devices  13.5 us (7%)
  blocking collectives  10.1 us (5%)
  other arithmetic  5.23 us (3%)
    psum x1, waiting for transfers between devices, on_device(): summed = lax.psum(local_grad, 'tm')  69 us
    reduce_scatter x1, waiting for transfers between devices, on_device(): owned = lax.psum_scatter(summed, 'clip', scatter_dimension=1, tiled=True)  20 us
    dot_general x12, matrix products, transpose_dot(): lax.dot_general(left, right, (((1,), (1,)), ((), ())), preferred_element_...  12.3 us
    ppermute x2, starting transfers between devices, padded_2(): lax.ppermute(tail, axis, [(i, (i + 1) % count) for i in range(ends)])  10.8 us
    all_gather x1, blocking collectives, on_device(): lax.all_gather(temporal_b, 'clip', axis=1, tiled=True)  10.1 us
    dot_general x9, matrix products, on_device(): jnp.dot(window, spatial_all[3 * shift_y + shift_x], preferred_element_typ...  7.74 us
    ppermute x2, waiting for transfers between devices, padded_2(): lax.ppermute(tail, axis, [(i, (i + 1) % count) for i in range(ends)])  4.81 us
    all_gather x1, waiting for transfers between devices, on_device(): lax.all_gather(spatial_w, 'clip', axis=1, tiled=True)  4.46 us
  transfers between devices with their start and end apart: 7, of which 5 were waited for; matrix products, arithmetic and copies ran while one was open for 23% of the time, Pallas kernels for 0%

commit v1 on v0

--- a/solution.py
+++ b/solution.py
@@ -76,7 +76,8 @@
         grads.append(outer_dot(shifted_hid, cot_flat))
     local_grad = jnp.stack(grads)
     total_rows = row_count * lax.axis_size("tm") * lax.axis_size("clip")
-    summed = lax.psum(local_grad, "tm")
+    after = lax.all_gather(local_grad, axis_name="tm")
+    summed = jnp.sum(after, axis=0)
     owned = lax.psum_scatter(summed, "clip", scatter_dimension=1, tiled=True)
     grad_temporal = owned * (1.0 / math.sqrt(total_rows))
     grad_spatial = (grad_hidden * sigmoid_s * (1.0 + spatial * (1.0 - sigmoid_s))).astype(

time: 186 us -> 278 us (1.49)
  waiting for transfers between devices: 99 us -> 192 us
  other arithmetic: 5.23 us -> 13.9 us
  matrix products: 27.1 us -> 21.9 us
    all_gather x0 -> x1, waiting for transfers between devices: none -> 131 us  [on_device(): after = lax.all_gather(local_grad, axis_name='tm')]
    psum x1 -> x0, waiting for transfers between devices: 69 us -> none  [on_device(): summed = lax.psum(local_grad, 'tm')]
    all_gather x1, waiting for transfers between devices: 4.46 us -> 24.8 us  [on_device(): lax.all_gather(spatial_w, 'clip', axis=1, tiled=True)]
    ppermute x2, waiting for transfers between devices: 4.81 us -> 15.6 us  [padded_2(): lax.ppermute(tail, axis, [(i, (i + 1) % count) for i in range(ends)])]
    reduce_scatter x1, waiting for transfers between devices: 20 us -> 13.4 us  [on_device(): owned = lax.psum_scatter(summed, 'clip', scatter_dimension=1, tiled=True)]
    reduce_sum x0 -> x1, other arithmetic: none -> 6.42 us  [on_device(): summed = jnp.sum(after, axis=0)]
    ppermute x2, waiting for transfers between devices: 0.01 us -> 5.96 us  [padded_2(): lax.ppermute(head, axis, [((i + 1) % count, i) for i in range(ends)])]
  transfers between devices with their start and end apart: 7 -> 7, of which waited for: 5 -> 6; matrix products, arithmetic and copies ran while one was open for 23% -> 12% of each run, Pallas kernels for 0% -> 0%
where the time goes in v1:
time: 278 us; the launch traced here: 277 us
  waiting for transfers between devices  192 us (69%)
  matrix products  21.9 us (8%)
  local copies, waits for them, and re-layouts  15.6 us (6%)
  between operations  14.1 us (5%)
  other arithmetic  13.9 us (5%)
  starting transfers between devices  12.3 us (4%)
  blocking collectives  7.78 us (3%)
    all_gather x1, waiting for transfers between devices, on_device(): after = lax.all_gather(local_grad, axis_name='tm')  131 us
    all_gather x1, waiting for transfers between devices, on_device(): lax.all_gather(spatial_w, 'clip', axis=1, tiled=True)  24.8 us
    ppermute x2, waiting for transfers between devices, padded_2(): lax.ppermute(tail, axis, [(i, (i + 1) % count) for i in range(ends)])  15.6 us
    reduce_scatter x1, waiting for transfers between devices, on_device(): owned = lax.psum_scatter(summed, 'clip', scatter_dimension=1, tiled=True)  13.4 us
    dot_general x12, matrix products, transpose_dot(): lax.dot_general(left, right, (((1,), (1,)), ((), ())), preferred_element_...  12.4 us
    ppermute x2, starting transfers between devices, padded_2(): lax.ppermute(tail, axis, [(i, (i + 1) % count) for i in range(ends)])  9.6 us
    all_gather x1, blocking collectives, on_device(): lax.all_gather(temporal_b, 'clip', axis=1, tiled=True)  7.78 us
    dot_general x9, matrix products, on_device(): jnp.dot(window, spatial_all[3 * shift_y + shift_x], preferred_element_typ...  6.49 us
  transfers between devices with their start and end apart: 7, of which 6 were waited for; matrix products, arithmetic and copies ran while one was open for 12% of the time, Pallas kernels for 0%

profile of v1, /device:TPU:0, one launch (start us, length us, event | category | flops | bytes accessed | tf_op | source)
XLA Modules:
  0.0 277.1 jit_solution(17036696377614891153)
XLA Ops:
  9.1 1.6 pad_slice_fusion.8
  10.7 24.8 %all-gather.4.cloned.1.call-done = bf16[9,320,320]{2,1,0:T(8,128)(2,1)} async-done(((bf16[9,80,320]{2,1,0:T(8,128)(2,1)}), bf16[9,320,320]{2,1,0:T(8,128)(2,1)}) %all-gather.4.cloned.1.call-update) | async-done | bytes 1843216 | tf_op jit(solution)/shard_map/all_gather | solution.py:44
  35.5 1.5 fusion.14
  37.0 1.5 convolution_add_fusion.14
  41.3 1.3 multiply_convert_fusion
  43.5 1.3 collective-permute-start.1
  46.0 4.6 %collective-permute-start = (bf16[1,1,16,32,320]{4,3,2,1,0:T(8,128)(2,1)}, bf16[1,1,16,32,320]{4,3,2,1,0:T(8,128)(2,1)S(1)}, u32[]{:S(2)}, u32[]{:S(2)}) collective-permute-start(bf16[1,1,16,32,320]{4,3,2,1,0:T(8,128)(2,1)} %bitcast.18), channel_id=1, source_target_pairs={{0,4},{4,8},{8,12},{12,16},{16,20},{20,24},{24,28},{1,5},{5,9},{9,... | collective-permute-start | bytes 983048 | tf_op jit(solution)/shard_map/ppermute | solution.py:16
  50.9 6.0 %collective-permute-done.1 = bf16[1,1,16,32,320]{4,3,2,1,0:T(8,128)(2,1)S(1)} collective-permute-done((bf16[1,1,16,32,320]{4,3,2,1,0:T(8,128)(2,1)}, bf16[1,1,16,32,320]{4,3,2,1,0:T(8,128)(2,1)S(1)}, u32[]{:S(2)}, u32[]{:S(2)}) %collective-permute-start.1) | collective-permute-done | bytes 327712 | tf_op jit(solution)/shard_map/ppermute | solution.py:18
  57.2 8.0 %collective-permute-done = bf16[1,1,16,32,320]{4,3,2,1,0:T(8,128)(2,1)S(1)} collective-permute-done((bf16[1,1,16,32,320]{4,3,2,1,0:T(8,128)(2,1)}, bf16[1,1,16,32,320]{4,3,2,1,0:T(8,128)(2,1)S(1)}, u32[]{:S(2)}, u32[]{:S(2)}) %collective-permute-start) | collective-permute-done | bytes 327712 | tf_op jit(solution)/shard_map/ppermute | solution.py:16
  65.6 1.3 pad_maximum_fusion
  67.0 5.0 %collective-permute-start.3 = (bf16[1,1,16,32,320]{4,3,2,1,0:T(8,128)(2,1)S(1)}, bf16[1,1,16,32,320]{4,3,2,1,0:T(8,128)(2,1)}, u32[]{:S(2)}, u32[]{:S(2)}) collective-permute-start(bf16[1,1,16,32,320]{4,3,2,1,0:T(8,128)(2,1)S(1)} %convert_element_type.21), channel_id=1, source_target_pairs={{0,4},{4,8},{8,12},{12,16},{16,20},{20,24},{24,28},{1,5},{5,9},{9,... | collective-permute-start | bytes 983048 | tf_op jit(solution)/shard_map/ppermute | solution.py:16
  74.4 7.8 %all_gather.13 = bf16[3,320,320]{2,1,0:T(8,128)(2,1)S(1)} all-gather(bf16[3,80,320]{2,1,0:T(8,128)(2,1)S(1)} %convert_element_type.20), channel_id=1, replica_groups=mesh['tm'=8,'clip'=4] {'clip'}, dimensions={1}, use_global_device_ids=true | all-gather | bytes 768000 | tf_op jit(solution)/shard_map/all_gather | solution.py:45
  83.3 2.3 copy.21
  85.6 7.6 %collective-permute-done.3 = bf16[1,1,16,32,320]{4,3,2,1,0:T(8,128)(2,1)} collective-permute-done((bf16[1,1,16,32,320]{4,3,2,1,0:T(8,128)(2,1)S(1)}, bf16[1,1,16,32,320]{4,3,2,1,0:T(8,128)(2,1)}, u32[]{:S(2)}, u32[]{:S(2)}) %collective-permute-start.3) | collective-permute-done | bytes 327712 | tf_op jit(solution)/shard_map/ppermute | solution.py:16
  93.2 1.4 fusion.21
  94.6 1.9 fusion.9
  97.4 4.5 %pad_slice_fusion.4 = (bf16[1,1,16,32,320]{4,3,2,1,0:T(8,128)(2,1)}, bf16[1,1,16,32,320]{4,3,2,1,0:T(8,128)(2,1)}, bf16[1,1,16,32,320]{4,3,2,1,0:T(8,128)(2,1)},...) fusion(bf16[1,1,16,32,320]{4,3,2,1,0:T(8,128)(2,1)} %bitcast.134), kind=kLoop, calls=%fused_computation.35 | loop fusion | bytes 2949120 | tf_op jit(solution)/shard_map/slice | solution.py:93
  105.6 131.1 %all-gather.6.cloned.1.call-done = f32[24,320,320]{2,1,0:T(8,128)} async-done(((f32[3,320,320]{2,1,0:T(8,128)}), f32[24,320,320]{2,1,0:T(8,128)}) %all-gather.6.cloned.1.call-update) | async-done | bytes 9830416 | tf_op jit(solution)/shard_map/all_gather | solution.py:79
  236.6 6.4 %reduce_sum.9 = f32[3,320,320]{2,1,0:T(8,128)} reduce(f32[8,3,320,320]{3,2,1,0:T(8,128)} %bitcast.123, f32[]{:T(128)} %constant.3.clone.1), dimensions={0}, to_apply=%region_0.1 | reduce | flops 2150400 | bytes 11059204 | tf_op jit(solution)/shard_map/reduce_sum | solution.py:80
  243.5 1.6 convolution_add_fusion.4
  248.5 2.4 copy.22
  253.1 1.3 copy.19
  255.4 13.4 %reduce-scatter.2.cloned.1.call-done = f32[3,80,320]{2,1,0:T(8,128)} async-done(((f32[3,320,320]{2,1,0:T(8,128)}), f32[3,80,320]{2,1,0:T(8,128)}) %reduce-scatter.2.cloned.1.call-update) | async-done | bytes 307216 | tf_op jit(solution)/shard_map/reduce_scatter | solution.py:81
  268.8 1.7 broadcast_multiply_fusion
  (79 shorter events, 22.9 us)
Async XLA Ops:
  7.2 28.3 %all-gather.4.cloned.1.call-start = ((), (), s32[]{:S(2)}) async-start(), calls=%async_computation.1 | async-start | bytes 2764800 | tf_op jit(solution)/shard_map/all_gather | solution.py:44
  7.9 228.7 %all-gather.6.cloned.1.call-start = ((), (), s32[]{:S(2)}) async-start(), calls=%async_computation.3 | async-start | bytes 13271040 | tf_op jit(solution)/shard_map/all_gather | solution.py:79
  35.5 3.0 %copy-start = (bf16[9,320,320]{2,1,0:T(8,128)(2,1)S(1)}, bf16[9,320,320]{2,1,0:T(8,128)(2,1)}, u32[]{:S(2)}) copy-start(bf16[9,320,320]{2,1,0:T(8,128)(2,1)} %all-gather.4.cloned.1.call-done) | copy-start | bytes 5529604
  35.5 3.0 %copy-start.13 = (bf16[1,1,16,32,320]{4,3,2,1,0:T(8,128)(2,1)S(1)}, bf16[1,1,16,32,320]{4,3,2,1,0:T(8,128)(2,1)}, u32[]{:S(2)}) copy-start(bf16[1,1,16,32,320]{4,3,2,1,0:T(8,128)(2,1)} %get-tuple-element.16) | copy-start | bytes 983044
  37.0 1.9 copy-start.12
  39.3 1.0 copy-start.10
  40.3 1.0 copy-start.18
  42.6 14.6 %copy-start.2 = (bf16[512,320]{0,1:T(8,128)(2,1)}, bf16[512,320]{0,1:T(8,128)(2,1)S(1)}, u32[]{:S(2)}) copy-start(bf16[512,320]{0,1:T(8,128)(2,1)S(1)} %get-tuple-element.22) | copy-start | bytes 983044
  43.5 13.3 %collective-permute-start.1 = (bf16[1,1,16,32,320]{4,3,2,1,0:T(8,128)(2,1)}, bf16[1,1,16,32,320]{4,3,2,1,0:T(8,128)(2,1)S(1)}, u32[]{:S(2)}, u32[]{:S(2)}) collective-permute-start(bf16[1,1,16,32,320]{4,3,2,1,0:T(8,128)(2,1)} %bitcast.18), channel_id=1, source_target_pairs={{4,0},{8,4},{12,8},{16,12},{20,16},{24,20},{28,24},{5,1},{9,5},{13... | collective-permute-start | bytes 983048 | tf_op jit(solution)/shard_map/ppermute | solution.py:18
  46.0 19.3 %collective-permute-start = (bf16[1,1,16,32,320]{4,3,2,1,0:T(8,128)(2,1)}, bf16[1,1,16,32,320]{4,3,2,1,0:T(8,128)(2,1)S(1)}, u32[]{:S(2)}, u32[]{:S(2)}) collective-permute-start(bf16[1,1,16,32,320]{4,3,2,1,0:T(8,128)(2,1)} %bitcast.18), channel_id=1, source_target_pairs={{0,4},{4,8},{8,12},{12,16},{16,20},{20,24},{24,28},{1,5},{5,9},{9,... | collective-permute-start | bytes 983048 | tf_op jit(solution)/shard_map/ppermute | solution.py:16
  56.8 8.4 %copy-start.19 = (bf16[1,1,16,32,320]{4,3,2,1,0:T(8,128)(2,1)}, bf16[1,1,16,32,320]{4,3,2,1,0:T(8,128)(2,1)S(1)}, u32[]{:S(2)}) copy-start(bf16[1,1,16,32,320]{4,3,2,1,0:T(8,128)(2,1)S(1)} %collective-permute-done.1) | copy-start | bytes 983044
  65.2 1.7 copy-start.16
  66.9 201.9 %reduce-scatter.2.cloned.1.call-start = ((), (), s32[]{:S(2)}) async-start(), calls=%async_computation.2 | async-start | bytes 1843200 | tf_op jit(solution)/shard_map/reduce_scatter | solution.py:81
  67.0 26.2 %collective-permute-start.3 = (bf16[1,1,16,32,320]{4,3,2,1,0:T(8,128)(2,1)S(1)}, bf16[1,1,16,32,320]{4,3,2,1,0:T(8,128)(2,1)}, u32[]{:S(2)}, u32[]{:S(2)}) collective-permute-start(bf16[1,1,16,32,320]{4,3,2,1,0:T(8,128)(2,1)S(1)} %convert_element_type.21), channel_id=1, source_target_pairs={{0,4},{4,8},{8,12},{12,16},{16,20},{20,24},{24,28},{1,5},{5,9},{9,... | collective-permute-start | bytes 983048 | tf_op jit(solution)/shard_map/ppermute | solution.py:16
  72.0 22.6 %collective-permute-start.2 = (bf16[1,1,16,32,320]{4,3,2,1,0:T(8,128)(2,1)S(1)}, bf16[1,1,16,32,320]{4,3,2,1,0:T(8,128)(2,1)}, u32[]{:S(2)}, u32[]{:S(2)}) collective-permute-start(bf16[1,1,16,32,320]{4,3,2,1,0:T(8,128)(2,1)S(1)} %convert_element_type.21), channel_id=1, source_target_pairs={{4,0},{8,4},{12,8},{16,12},{20,16},{24,20},{28,24},{5,1},{9,5},{13... | collective-permute-start | bytes 983048 | tf_op jit(solution)/shard_map/ppermute | solution.py:18
  243.1 2.0 copy-start.9
  243.5 2.1 copy-start.8
  245.5 1.1 copy-start.4
  245.5 1.3 copy-start.5
  245.5 1.7 copy-start.6
  245.5 1.8 copy-start.15
  247.3 3.6 %copy-start.3 = (bf16[512,320]{0,1:T(8,128)(2,1)S(1)}, bf16[512,320]{0,1:T(8,128)(2,1)}, u32[]{:S(2)}) copy-start(bf16[512,320]{0,1:T(8,128)(2,1)} %copy-done.2) | copy-start | bytes 983044
  248.5 2.8 copy-start.20
  251.7 2.8 %copy-start.1 = (f32[1,1,16,32,320]{4,3,2,1,0:T(8,128)S(1)}, f32[1,1,16,32,320]{4,3,2,1,0:T(8,128)}, u32[]{:S(2)}) copy-start(f32[1,1,16,32,320]{4,3,2,1,0:T(8,128)} %param.5) | copy-start | bytes 1966084
  (5 other events, 4.9 us)
Sparse Core Ops, SparseCore 0:
  9.5 25.9 all-gather.3
  67.1 169.5 all-gather.5
  243.2 25.6 reduce-scatter.1
